TPU v7x, 32 devices: a whole 2x2x4 slice. The times are simulated.
32 devices in a mesh: groups: 2 (over y), patch: 4 (over z), head: 4 (over x, core).
Axes of the slice: x: 2, y: 2, z: 4, core: 2. Of those that a mesh axis runs over, the one named last changes fastest.
Arguments:
- queries: bfloat16 [1536, 1536], P(('groups', 'patch'), 'head'), parts along dimension 0, may hold values from -12.5 to 12.5
- fresh_keys: bfloat16 [1536, 1536], P(('groups', 'patch'), 'head'), parts along dimension 0, may hold values from -5 to 5
- fresh_values: bfloat16 [1536, 1536], P(('groups', 'patch'), 'head'), parts along dimension 0, may hold values from -6 to 6
- stale_keys: bfloat16 [1536, 1536], P(('groups', 'patch'), 'head'), parts along dimension 0, may hold values from -5 to 5
- stale_values: bfloat16 [1536, 1536], P(('groups', 'patch'), 'head'), parts along dimension 0, may hold values from -6 to 6
- out_weight: bfloat16 [1536, 5120], P('head', 'patch'), may hold values from -0.21875 to 0.21875
- gate_scale: float32 [10240], P(('groups', 'head')), parts along dimension 0, may hold values from 1 to 4
Outputs:
- branch_out: float32 [1536, 5120], P(('groups', 'patch'), 'head'), parts along dimension 0
There are 2 independent parts, one for each index of `groups`. A program takes and returns all parts, laid end to end along the dimension named above; an argument that names none is the same for every part. Nothing has to cross between parts.
All inputs are finite; a program needn't handle non-finite values.
Results may differ from a plain program's by a relative error of at most 0.006.
Values may be sent and summed in bfloat16 or wider, within the bound.
No kernel may reach another device: no remote copies, remote signals or barrier semaphores. Data moves between devices by JAX's collectives and lax.ppermute only.
A program may use at most 64 MiB of HBM per device.

v0:
```python
import jax
import jax.numpy as jnp
from jax import lax
from jax.sharding import PartitionSpec as P

HEAD_DIM = 128


neg_large = -1e30


def head_view(matrix):
    return matrix.reshape(matrix.shape[0], -1, HEAD_DIM)


def block_scores(query_heads, key_block):
    return jnp.einsum(
        "qhd,khd->hqk", query_heads, head_view(key_block), preferred_element_type=jnp.float32
    ) * HEAD_DIM ** (-0.5)


def absorb(running, scores, value_block):
    run_max, run_total, run_acc = running
    new_max = jnp.maximum(run_max, jnp.max(scores, axis=2))
    factor = jnp.exp(run_max - new_max)
    weights = jnp.exp(scores - new_max[:, :, None])
    new_total = run_total * factor + jnp.sum(weights, axis=2)
    mixture = jnp.einsum(
        "hqk,khd->qhd",
        weights.astype(jnp.bfloat16),
        head_view(value_block),
        preferred_element_type=jnp.float32,
    )
    new_acc = run_acc * jnp.transpose(factor)[:, :, None] + mixture
    return (new_max, new_total, new_acc)


def empty_state(row_count, head_count):
    return (
        jnp.full((head_count, row_count), neg_large, jnp.float32),
        jnp.zeros((head_count, row_count), jnp.float32),
        jnp.zeros((row_count, head_count, HEAD_DIM), jnp.float32),
    )


def on_device(queries, fresh_keys, fresh_values, stale_keys, stale_values, out_weight, gate_scale):
    query_heads = head_view(queries)
    row_count = query_heads.shape[0]
    head_count = query_heads.shape[1]
    own_index = lax.axis_index("patch")
    own_start = own_index * row_count
    local = absorb(
        empty_state(row_count, head_count), block_scores(query_heads, fresh_keys), fresh_values
    )
    key_piece = lax.all_gather(stale_keys, "patch", axis=0, tiled=True)
    value_piece = lax.all_gather(stale_values, "patch", axis=0, tiled=True)
    key_count = key_piece.shape[0]
    key_step = 1024 if key_count > 1024 and key_count % 1024 == 0 else key_count

    def visit(block_index, inner):
        offset = block_index * key_step
        key_block = lax.dynamic_slice_in_dim(key_piece, offset, key_step, 0)
        value_block = lax.dynamic_slice_in_dim(value_piece, offset, key_step, 0)
        scores = block_scores(query_heads, key_block)
        position = offset + lax.iota(jnp.int32, key_step)
        own_rows = (position >= own_start) & (position < own_start + row_count)
        scores = jnp.where(own_rows[None, None, :], neg_large, scores)
        return absorb(inner, scores, value_block)

    run_max, run_total, run_acc = lax.fori_loop(0, key_count // key_step, visit, local)
    attended = (
        (run_acc / jnp.transpose(run_total)[:, :, None]).astype(jnp.bfloat16).reshape(row_count, -1)
    )
    partial_out = jnp.dot(
        attended,
        lax.all_gather(out_weight, "patch", axis=1, tiled=True),
        preferred_element_type=jnp.float32,
    )
    summed = lax.psum_scatter(partial_out, "head", scatter_dimension=1, tiled=True)
    return gate_scale[None, :] * summed


def solution(mesh):
    return jax.shard_map(
        on_device,
        mesh=mesh,
        in_specs=(
            P(("groups", "patch"), "head"),
            P(("groups", "patch"), "head"),
            P(("groups", "patch"), "head"),
            P(("groups", "patch"), "head"),
            P(("groups", "patch"), "head"),
            P("head", "patch"),
            P(("groups", "head")),
        ),
        out_specs=P(("groups", "patch"), "head"),
        check_vma=False,
    )
```

profile of v0, /device:TPU:1, one launch (start us, length us, event | category | flops | bytes accessed | tf_op | source)
XLA Modules:
  0.0 154.1 jit_solution(16892380855673942393)
XLA Ops:
  6.5 0.0 copy-start
  6.5 0.0 copy-start.2
  6.5 0.0 all-gather.2.cloned.1.call-start
  6.5 0.7 all-gather.2.cloned.1.call-update
  7.3 0.0 reduce-scatter.2.cloned.1.call-start
  7.3 0.0 copy-start.1
  7.3 16.1 %all_gather.9 = bf16[768,384]{1,0:T(8,128)(2,1)S(1)} all-gather(bf16[192,384]{1,0:T(8,128)(2,1)} %param.10), channel_id=1, replica_groups=mesh['groups'=2,'patch'=4,'head'=4] {'patch'}, dimensions={0}, use_global_device_ids=true | all-gather | bytes 737280 | tf_op jit(solution)/shard_map/all_gather | solution.py:55
  23.4 0.3 copy.27
  23.6 0.0 copy-done.2
  23.7 22.3 %all_gather.10 = bf16[768,384]{1,0:T(8,128)(2,1)S(1)} all-gather(bf16[192,384]{1,0:T(8,128)(2,1)S(1)} %copy-done.2), channel_id=1, replica_groups=mesh['groups'=2,'patch'=4,'head'=4] {'patch'}, dimensions={0}, use_global_device_ids=true | all-gather | bytes 737280 | tf_op jit(solution)/shard_map/all_gather | solution.py:56
  45.9 0.3 copy.30
  46.2 0.0 copy-done
  46.2 0.0 copy-done.1
  46.2 0.3 fusion.39
  46.5 0.5 fusion
  47.0 0.1 fusion.14
  47.1 0.5 fusion.1
  47.7 0.0 copy-start.4
  47.7 0.6 convolution_bitcast_fusion.1
  48.3 0.3 copy-done.4
  48.6 0.5 fusion.8
  49.0 49.3 %all-gather.2.cloned.1.call-done = bf16[384,5120]{1,0:T(8,128)(2,1)} async-done(((bf16[384,1280]{1,0:T(8,128)(2,1)}), bf16[384,5120]{1,0:T(8,128)(2,1)}) %all-gather.2.cloned.1.call-update) | async-done | bytes 3932176 | tf_op jit(solution)/shard_map/all_gather | solution.py:76
  98.4 5.2 %fusion.18 = f32[192,5120]{1,0:T(8,128)} fusion(bf16[384,5120]{1,0:T(8,128)(2,1)} %all-gather.2.cloned.1.call-done, bf16[3,24,8,128]{3,2,1,0:T(8,128)(2,1)S(1)} %fusion.8), kind=kOutput, calls=%fused_computation.23 | convolution fusion | flops 754974720 | bytes 8011776 | tf_op jit(solution)/shard_map/dot_general | solution.py:74
  103.5 0.0 copy-start.3
  103.5 0.0 reduce-scatter.2.cloned.1.call-update
  103.6 41.5 %reduce-scatter.2.cloned.1.call-done = f32[192,1280]{1,0:T(8,128)} async-done(((f32[192,5120]{1,0:T(8,128)}), f32[192,1280]{1,0:T(8,128)}) %reduce-scatter.2.cloned.1.call-update) | async-done | bytes 983056 | tf_op jit(solution)/shard_map/reduce_scatter | solution.py:79
  145.0 0.0 copy-done.3
  145.0 2.2 %broadcast_multiply_fusion = f32[192,1280]{1,0:T(8,128)} fusion(f32[192,1280]{1,0:T(8,128)} %reduce-scatter.2.cloned.1.call-done, f32[1280]{0:T(1024)S(1)} %copy-done.3), kind=kLoop, calls=%fused_computation.21 | loop fusion | flops 245760 | bytes 1971200 | tf_op jit(solution)/shard_map/mul | solution.py:80
  (3 shorter events, 0.0 us)
Async XLA Ops:
  6.5 39.7 %copy-start = (bf16[192,384]{1,0:T(8,128)(2,1)S(1)}, bf16[192,384]{1,0:T(8,128)(2,1)}, u32[]{:S(2)}) copy-start(bf16[192,384]{1,0:T(8,128)(2,1)} %param.7) | copy-start | bytes 442372
  6.5 17.1 %copy-start.2 = (bf16[192,384]{1,0:T(8,128)(2,1)S(1)}, bf16[192,384]{1,0:T(8,128)(2,1)}, u32[]{:S(2)}) copy-start(bf16[192,384]{1,0:T(8,128)(2,1)} %param.11) | copy-start | bytes 442372
  6.5 91.8 %all-gather.2.cloned.1.call-start = ((), (), s32[]{:S(2)}) async-start(), calls=%async_computation.1 | async-start | bytes 4915200 | tf_op jit(solution)/shard_map/all_gather | solution.py:76
  7.3 137.8 %reduce-scatter.2.cloned.1.call-start = ((), (), s32[]{:S(2)}) async-start(), calls=%async_computation.2 | async-start | bytes 4915200 | tf_op jit(solution)/shard_map/reduce_scatter | solution.py:79
  7.3 38.9 %copy-start.1 = (bf16[192,384]{1,0:T(8,128)(2,1)S(1)}, bf16[192,384]{1,0:T(8,128)(2,1)}, u32[]{:S(2)}) copy-start(bf16[192,384]{1,0:T(8,128)(2,1)} %param.8) | copy-start | bytes 442372
  47.7 0.9 copy-start.4
  103.5 41.5 %copy-start.3 = (f32[1280]{0:T(1024)S(1)}, f32[1280]{0:T(1024)}, u32[]{:S(2)}) copy-start(f32[1280]{0:T(1024)} %param.13) | copy-start | bytes 15364
Sparse Core Ops, SparseCore 0:
  8.9 89.4 all-gather.1
  103.7 41.2 reduce-scatter.1
where the time goes:
time: 155 us; the launch traced here: 154 us
  waiting for transfers between devices  91.5 us (59%)
  blocking collectives  38.3 us (25%)
  between operations  13.5 us (9%)
  matrix products  6.96 us (4%)
  other arithmetic  2.89 us (2%)
    all_gather x1, waiting for transfers between devices, on_device(): lax.all_gather(out_weight, 'patch', axis=1, tiled=True)  49.3 us
    reduce_scatter x1, waiting for transfers between devices, on_device(): lax.psum_scatter(partial_out, 'head', scatter_dimension=1, tiled=True)  41.5 us
    all_gather x1, blocking collectives, on_device(): value_piece = lax.all_gather(stale_values, 'patch', axis=0, tiled=True)  22.3 us
    all_gather x1, blocking collectives, on_device(): key_piece = lax.all_gather(stale_keys, 'patch', axis=0, tiled=True)  16.1 us
    dot_general x1, matrix products, on_device(): jnp.dot(attended, lax.all_gather(out_weight, 'patch', axis=1, tiled=True)...  5.17 us
  transfers between devices with their start and end apart: 2, of which 2 were waited for; matrix products, arithmetic and copies ran while one was open for 2% of the time, Pallas kernels for 0%

commit v1 on v0

v1 whole, which is shorter than its diff:
```python
import functools

import jax
import jax.numpy as jnp
from jax import lax
from jax.experimental import pallas as pl
from jax.experimental.pallas import tpu as pltpu
from jax.sharding import PartitionSpec as P

HEAD_DIM = 128
MASKED = -1e30


def absorb(query, state, key, value, bias):
    scores = lax.dot_general(
        query, key, (((1,), (1,)), ((), ())), preferred_element_type=jnp.float32
    ) * HEAD_DIM ** (-0.5)
    if bias is not None:
        scores = scores + bias
    block_top = jnp.max(scores, axis=1, keepdims=True)
    top = block_top if state is None else jnp.maximum(state[0], block_top)
    weights = jnp.exp(scores - top)
    total = jnp.sum(weights, axis=1, keepdims=True)
    mixture = jnp.dot(
        weights.astype(jnp.bfloat16), value, preferred_element_type=jnp.float32
    )
    if state is not None:
        factor = jnp.exp(state[0] - top)
        total = total + state[1] * factor
        mixture = mixture + state[2] * factor
    return top, total, mixture


def head_columns(head):
    return slice(head * HEAD_DIM, (head + 1) * HEAD_DIM)


def first_kernel(count, bias_ref, q_ref, key_ref, value_ref, *refs):
    blocks, (top_ref, total_ref, mix_ref) = refs[:count], refs[count:]
    width = q_ref.shape[1]
    for head in range(width // HEAD_DIM):
        cols = head_columns(head)
        query = q_ref[:, cols]
        state = absorb(query, None, key_ref[:, cols], value_ref[:, cols], None)
        for index, block in enumerate(blocks):
            high = slice(width + head * HEAD_DIM, width + (head + 1) * HEAD_DIM)
            state = absorb(query, state, block[:, cols], block[:, high], bias_ref[index])
        top_ref[head], total_ref[head], mix_ref[:, cols] = state


def last_kernel(count, bias_ref, q_ref, top_ref, total_ref, mix_ref, *refs):
    blocks, (out_ref,) = refs[:count], refs[count:]
    width = q_ref.shape[1]
    for head in range(width // HEAD_DIM):
        cols = head_columns(head)
        query = q_ref[:, cols]
        state = (top_ref[head], total_ref[head], mix_ref[:, cols])
        for index, block in enumerate(blocks):
            high = slice(width + head * HEAD_DIM, width + (head + 1) * HEAD_DIM)
            state = absorb(query, state, block[:, cols], block[:, high], bias_ref[index])
        out_ref[:, cols] = (state[2] / state[1]).astype(out_ref.dtype)


def attention_cost(rows, width, keys):
    return pl.CostEstimate(
        flops=4 * rows * width * keys,
        transcendentals=rows * keys * (width // HEAD_DIM),
        bytes_accessed=4 * keys * width,
    )


SMEM = pl.BlockSpec(memory_space=pltpu.SMEM)
VMEM = pl.BlockSpec(memory_space=pltpu.VMEM)
PARAMS = pltpu.CompilerParams(vmem_limit_bytes=20 * 2**20)


def attend_first(queries, keys, values, blocks, bias):
    rows, width = queries.shape
    heads = width // HEAD_DIM
    count = len(blocks)
    narrow = jax.ShapeDtypeStruct((heads, rows, 1), jnp.float32)
    return pl.pallas_call(
        functools.partial(first_kernel, count),
        out_shape=(narrow, narrow, jax.ShapeDtypeStruct((rows, width), jnp.float32)),
        in_specs=[SMEM] + [VMEM] * (3 + count),
        out_specs=(VMEM, VMEM, VMEM),
        cost_estimate=attention_cost(rows, width, rows * (count + 1)),
        compiler_params=PARAMS,
        name="attend_first",
    )(bias, queries, keys, values, *blocks)


def attend_last(queries, state, blocks, bias):
    rows, width = queries.shape
    count = len(blocks)
    return pl.pallas_call(
        functools.partial(last_kernel, count),
        out_shape=jax.ShapeDtypeStruct((rows, width), jnp.bfloat16),
        in_specs=[SMEM] + [VMEM] * (4 + count),
        out_specs=VMEM,
        cost_estimate=attention_cost(rows, width, rows * count),
        compiler_params=PARAMS,
        name="attend_last",
    )(bias, queries, *state, *blocks)


def project_kernel(count, *refs):
    left, right, out_ref = refs[:count], refs[count : 2 * count], refs[2 * count]
    total = jnp.dot(left[0][...], right[0][...], preferred_element_type=jnp.float32)
    for a_ref, w_ref in zip(left[1:], right[1:]):
        total = total + jnp.dot(a_ref[...], w_ref[...], preferred_element_type=jnp.float32)
    out_ref[...] = total.astype(out_ref.dtype)


def project(pieces, weights):
    rows, depth = pieces[0].shape
    columns = weights[0].shape[1]
    tile = 256 if columns % 256 == 0 else columns
    count = len(pieces)
    return pl.pallas_call(
        functools.partial(project_kernel, count),
        grid=(columns // tile,),
        out_shape=jax.ShapeDtypeStruct((rows, columns), jnp.bfloat16),
        in_specs=[pl.BlockSpec((rows, depth), lambda c: (0, 0))] * count
        + [pl.BlockSpec((depth, tile), lambda c: (0, c))] * count,
        out_specs=pl.BlockSpec((rows, tile), lambda c: (0, c)),
        cost_estimate=pl.CostEstimate(
            flops=2 * count * rows * depth * columns,
            transcendentals=0,
            bytes_accessed=2 * count * depth * columns,
        ),
        compiler_params=PARAMS,
        name="project",
    )(*pieces, *weights)


def gather_blocks(block, count):
    half = count // 2
    direct, passed = [], []
    middle = None
    if half:
        right = [(i, i + half) for i in range(count - half)]
        left = [(i, i - half) for i in range(half, count)]
        if 2 * half == count:
            middle = lax.ppermute(block, "patch", right + left)
            direct.append((middle, 0, count))
            held_right = held_left = middle
        else:
            held_right = lax.ppermute(block, "patch", right)
            held_left = lax.ppermute(block, "patch", left)
            direct += [(held_right, half, count), (held_left, 0, count - half)]
    for step in range(1, half):
        right = [(i, i + step) for i in range(count - step)]
        left = [(i, i - step) for i in range(step, count)]
        direct.append((lax.ppermute(block, "patch", right), step, count))
        direct.append((lax.ppermute(block, "patch", left), 0, count - step))
    for distance in range(half + 1, count):
        step = distance - half
        right = [(i, i + step) for i in range(half, count - step)]
        left = [(i, i - step) for i in range(step, count - half)]
        if 2 * half == count:
            block_far = lax.ppermute(middle, "patch", right + left)
            passed.append((block_far, distance, count - distance))
        else:
            passed.append((lax.ppermute(held_right, "patch", right), distance, count))
            passed.append((lax.ppermute(held_left, "patch", left), 0, count - distance))
    return direct, passed


def bias_of(ranges):
    index = lax.axis_index("patch")
    rows = []
    for _, first, last in ranges:
        if first < last:
            valid = (index >= first) & (index < last)
        else:
            valid = (index >= first) | (index < last)
        rows.append(jnp.where(valid, 0.0, MASKED).astype(jnp.float32))
    return jnp.stack(rows)


def on_device(n_patch, n_head, queries, fresh_keys, fresh_values, stale_keys, stale_values, out_weight, gate_scale):
    ratio = n_patch // n_head
    assert n_patch == ratio * n_head and n_head & (n_head - 1) == 0

    both = jnp.concatenate([stale_keys, stale_values], axis=1)
    direct, passed = gather_blocks(both, n_patch)

    weights = [out_weight]
    far = []
    bit = n_head // 2
    while bit > 1:
        pairs = [(i, i ^ bit) for i in range(n_head)]
        far.append((bit, pairs))
        bit //= 2
    held = {0: out_weight}
    for bit, pairs in far:
        held.update({k ^ bit: lax.ppermute(w, "head", pairs) for k, w in list(held.items())})

    state = attend_first(
        queries, fresh_keys, fresh_values, [b for b, _, _ in direct], bias_of(direct)
    )
    attended = attend_last(queries, state, [b for b, _, _ in passed], bias_of(passed))

    def spread(i):
        return (i % 2) * (n_head // 2) + i // 2

    def slab_of(p, i, s):
        b, q = divmod(p, ratio)
        return ((q + s) % ratio) * n_head + (b + spread(i)) % n_head

    places = [(p, i) for p in range(n_patch) for i in range(n_head)]

    pieces = [
        [
            lax.ppermute(
                attended,
                ("patch", "head"),
                [(slab_of(p, i, s) * n_head + (i ^ t), p * n_head + i) for p, i in places],
            )
            for t in range(n_head)
        ]
        for s in range(ratio)
    ]

    if n_head > 1:
        pairs = [(i, i ^ 1) for i in range(n_head)]
        late, attended = lax.optimization_barrier((held, attended))
        held = dict(late)
        held.update({k ^ 1: lax.ppermute(w, "head", pairs) for k, w in list(held.items())})
    weights = [held[t] for t in range(n_head)]

    results = []
    for s in range(ratio):
        block = project(pieces[s], weights)
        results.append(
            lax.ppermute(
                block,
                ("patch", "head"),
                [(p * n_head + i, slab_of(p, i, s) * n_head + p // ratio) for p, i in places],
            )
        )
    if ratio == 1:
        rows = results[0]
    else:
        own = lax.axis_index("patch") // n_head
        stacked = jnp.stack(results)
        order = (own - jnp.arange(ratio)) % ratio
        rows = jnp.concatenate([stacked[order[k]] for k in range(ratio)], axis=1)
    return gate_scale[None, :] * rows.astype(jnp.float32)


def solution(mesh):
    return jax.shard_map(
        functools.partial(on_device, mesh.shape["patch"], mesh.shape["head"]),
        mesh=mesh,
        in_specs=(
            P(("groups", "patch"), "head"),
            P(("groups", "patch"), "head"),
            P(("groups", "patch"), "head"),
            P(("groups", "patch"), "head"),
            P(("groups", "patch"), "head"),
            P("head", "patch"),
            P(("groups", "head")),
        ),
        out_specs=P(("groups", "patch"), "head"),
        check_vma=False,
    )
```

time: 155 us -> 70.3 us (0.45)
  waiting for transfers between devices: 91.5 us -> 39 us
  blocking collectives: 38.3 us -> 0 us
  starting transfers between devices: 0.04 us -> 23.3 us
  between operations: 13.5 us -> 0.17 us
  matrix products: 6.96 us -> 0 us
  Pallas kernels: 0 us -> 5.51 us
  other arithmetic: 2.89 us -> 1.09 us
    all_gather x1 -> x0, waiting for transfers between devices: 49.3 us -> none  [on_device(): lax.all_gather(out_weight, 'patch', axis=1, tiled=True)]
    reduce_scatter x1 -> x0, waiting for transfers between devices: 41.5 us -> none  [on_device(): lax.psum_scatter(partial_out, 'head', scatter_dimension=1, tiled=True)]
    ppermute x0 -> x12, waiting for transfers between devices: none -> 39 us  [the longest x1 13.8 us: on_device(): lax.ppermute(block, ('patch', 'head'), [(p * n_head + i, slab_of(p, i, s)...]
    all_gather x2 -> x0, blocking collectives: 38.3 us -> none  [the longest x1 22.3 us: on_device(): value_piece = lax.all_gather(stale_values, 'patch', axis=0, tiled=True)]
    ppermute x0 -> x12, starting transfers between devices: none -> 23.3 us  [the longest x4 6.82 us: on_device(): lax.ppermute(attended, ('patch', 'head'), [(slab_of(p, i, s) * n_head + (...]
    dot_general x5 -> x0, matrix products: 6.96 us -> none  [the longest x1 5.17 us: on_device(): jnp.dot(attended, lax.all_gather(out_weight, 'patch', axis=1, tiled=True)...]
    pallas_call x0 -> x3, Pallas kernels: none -> 5.51 us  [the longest x1 2.18 us: project(): pl.pallas_call(functools.partial(project_kernel, count), grid=(columns //...]
  transfers between devices with their start and end apart: 2 -> 12, of which waited for: 2 -> 6; matrix products, arithmetic and copies ran while one was open for 2% -> 2% of each run, Pallas kernels for 0% -> 5%
where the time goes in v1:
time: 70.3 us; the launch traced here: 70.1 us
  waiting for transfers between devices  39 us (55%)
  starting transfers between devices  23.3 us (33%)
  Pallas kernels  5.51 us (8%)
  other arithmetic  1.09 us (2%)
  local copies, waits for them, and re-layouts  1.02 us (1%)
    ppermute x1, waiting for transfers between devices, on_device(): lax.ppermute(block, ('patch', 'head'), [(p * n_head + i, slab_of(p, i, s)...  13.8 us
    ppermute x4, waiting for transfers between devices, on_device(): lax.ppermute(attended, ('patch', 'head'), [(slab_of(p, i, s) * n_head + (...  13.1 us
    ppermute x1, waiting for transfers between devices, gather_blocks(): middle = lax.ppermute(block, 'patch', right + left)  7.57 us
    ppermute x4, starting transfers between devices, on_device(): lax.ppermute(attended, ('patch', 'head'), [(slab_of(p, i, s) * n_head + (...  6.82 us
    ppermute x3, starting transfers between devices, on_device(): lax.ppermute(w, 'head', pairs)  5.65 us
    ppermute x1, waiting for transfers between devices, gather_blocks(): block_far = lax.ppermute(middle, 'patch', right + left)  4.44 us
    ppermute x1, starting transfers between devices, gather_blocks(): direct.append((lax.ppermute(block, 'patch', right), step, count))  4 us
    ppermute x1, starting transfers between devices, gather_blocks(): middle = lax.ppermute(block, 'patch', right + left)  2.37 us
  transfers between devices with their start and end apart: 12, of which 6 were waited for; matrix products, arithmetic and copies ran while one was open for 2% of the time, Pallas kernels for 5%

profile of v1, /device:TPU:1, one launch (start us, length us, event | category | flops | bytes accessed | tf_op | source)
XLA Modules:
  0.0 70.1 jit_solution(12044271930755675448)
XLA Ops:
  0.0 0.0 copy-start.4
  0.0 2.0 %collective-permute-start.8 = (bf16[384,1280]{1,0:T(8,128)(2,1)}, bf16[384,1280]{1,0:T(8,128)(2,1)S(1)}, u32[]{:S(2)}, u32[]{:S(2)}) collective-permute-start(bf16[384,1280]{1,0:T(8,128)(2,1)} %refs_4_), channel_id=1, source_target_pairs={{0,2},{1,3},{2,0},{3,1},{4,6},{5,7},{6,4},{7,5},{8,10},{9,11},{10,... | collective-permute-start | bytes 2949128 | tf_op jit(solution)/shard_map/ppermute | solution.py:198
  2.0 0.0 copy-start.3
  2.0 1.0 %constant_dynamic-update-slice_fusion.1 = bf16[192,768]{1,0:T(8,128)(2,1)S(1)} fusion(bf16[192,384]{1,0:T(8,128)(2,1)} %param.10), kind=kLoop, calls=%fused_computation.2 | loop fusion | bytes 294912
  3.0 0.0 copy-done.4
  3.0 0.0 copy-start.1
  3.0 0.0 copy-start.2
  3.1 2.4 %collective-permute-start = (bf16[192,768]{1,0:T(8,128)(2,1)S(1)}, bf16[192,768]{1,0:T(8,128)(2,1)S(1)}, u32[]{:S(2)}, u32[]{:S(2)}) collective-permute-start(bf16[192,768]{1,0:T(8,128)(2,1)S(1)} %constant_dynamic-update-slice_fusion), channel_id=1, source_target_pairs={{0,8},{4,12},{8,0},{12,4},{1,9},{5,13},{9,1},{13,5},{2,10},{6,14},... | collective-permute-start | bytes 884744 | tf_op jit(solution)/shard_map/ppermute | solution.py:145
  5.4 1.3 %collective-permute-start.2 = (bf16[192,768]{1,0:T(8,128)(2,1)S(1)}, bf16[192,768]{1,0:T(8,128)(2,1)S(1)}, u32[]{:S(2)}, u32[]{:S(2)}) collective-permute-start(bf16[192,768]{1,0:T(8,128)(2,1)S(1)} %constant_dynamic-update-slice_fusion), channel_id=1, source_target_pairs={{4,0},{8,4},{12,8},{5,1},{9,5},{13,9},{6,2},{10,6},{14,10},{7,3},{... | collective-permute-start | bytes 884744 | tf_op jit(solution)/shard_map/ppermute | solution.py:156
  6.7 4.0 %collective-permute-start.1 = (bf16[192,768]{1,0:T(8,128)(2,1)S(1)}, bf16[192,768]{1,0:T(8,128)(2,1)S(1)}, u32[]{:S(2)}, u32[]{:S(2)}) collective-permute-start(bf16[192,768]{1,0:T(8,128)(2,1)S(1)} %constant_dynamic-update-slice_fusion), channel_id=1, source_target_pairs={{0,4},{4,8},{8,12},{1,5},{5,9},{9,13},{2,6},{6,10},{10,14},{3,7},{... | collective-permute-start | bytes 884744 | tf_op jit(solution)/shard_map/ppermute | solution.py:155
  10.7 7.6 %collective-permute-done.refs_0_ = bf16[192,768]{1,0:T(8,128)(2,1)S(1)} collective-permute-done((bf16[192,768]{1,0:T(8,128)(2,1)S(1)}, bf16[192,768]{1,0:T(8,128)(2,1)S(1)}, u32[]{:S(2)}, u32[]{:S(2)}) %collective-permute-start) | collective-permute-done | bytes 294944 | tf_op jit(solution)/shard_map/ppermute | solution.py:145
  18.3 1.3 %collective-permute-start.3 = (bf16[192,768]{1,0:T(8,128)(2,1)S(1)}, bf16[192,768]{1,0:T(8,128)(2,1)S(1)}, u32[]{:S(2)}, u32[]{:S(2)}) collective-permute-start(bf16[192,768]{1,0:T(8,128)(2,1)S(1)} %collective-permute-done.refs_0_), channel_id=1, source_target_pairs={{8,12},{4,0},{9,13},{5,1},{10,14},{6,2},{11,15},{7,3},{24,28},{20,... | collective-permute-start | bytes 884744 | tf_op jit(solution)/shard_map/ppermute | solution.py:162
  19.6 0.1 pad_maximum_fusion.bias_ref
  19.7 0.0 collective-permute-done.2.refs_2_
  19.7 0.0 collective-permute-done.1.refs_1_
  19.7 0.0 copy-done.3
  19.7 0.0 copy-done.1
  19.7 0.0 copy-done.2
  19.7 2.0 %attend_first.1 = (f32[3,192,1]{2,1,0:T(8,128)S(1)}, f32[3,192,1]{2,1,0:T(8,128)S(1)}, f32[192,384]{1,0:T(8,128)S(1)}) custom-call(f32[3]{0:T(128)S(1)} %pad_maximum_fusion.bias_ref, bf16[192,384]{1,0:T(8,128)(2,1)S(1)} %copy-done.1, bf16[192,384]{1,0:T(8,128)(2,1)S(1)} %copy-done.2, bf16[192,384]{1,0:T(8,128)(2,1)S(1)} %copy-done.3, ...), custom_call_target="tpu_custom_call" | custom-call | flops 226492416 | bytes 1179648 | tf_op jit(solution)/shard_map/attend_first/pallas_call | solution.py:82
  21.7 0.0 copy-start
  21.7 4.4 %collective-permute-done.3.refs_0_ = bf16[192,768]{1,0:T(8,128)(2,1)S(1)} collective-permute-done((bf16[192,768]{1,0:T(8,128)(2,1)S(1)}, bf16[192,768]{1,0:T(8,128)(2,1)S(1)}, u32[]{:S(2)}, u32[]{:S(2)}) %collective-permute-start.3) | collective-permute-done | bytes 294944 | tf_op jit(solution)/shard_map/ppermute | solution.py:162
  26.1 1.4 %attend_last.1 = bf16[192,384]{1,0:T(8,128)(2,1)S(1)} custom-call(f32[1]{0:T(128)} %bitcast.bias_ref, bf16[192,384]{1,0:T(8,128)(2,1)S(1)} %copy-done.1, f32[3,192,1]{2,1,0:T(8,128)S(1)} %get-tuple-element.10.top_ref, f32[3,192,1]{2,1,0:T(8,128)S(1)} %get-tuple-element.11.total_ref, f32[192,384]{1,0:T(8,128)S(1)} %get-tuple-element.12.mix_ref, ...), custom_call_target="tpu_custom_call" | custom-call | flops 56623104 | bytes 294912 | tf_op jit(solution)/shard_map/attend_last/pallas_call | solution.py:96
  27.5 0.0 copy-start.5
  27.5 0.0 collective-permute-done.8.refs_6_
  27.5 0.0 copy-done
  27.5 3.5 %collective-permute-start.9 = (bf16[384,1280]{1,0:T(8,128)(2,1)S(1)}, bf16[384,1280]{1,0:T(8,128)(2,1)S(1)}, u32[]{:S(2)}, u32[]{:S(2)}) collective-permute-start(bf16[384,1280]{1,0:T(8,128)(2,1)S(1)} %copy-done), channel_id=1, source_target_pairs={{0,1},{1,0},{2,3},{3,2},{4,5},{5,4},{6,7},{7,6},{8,9},{9,8},{10,11... | collective-permute-start | bytes 2949128 | tf_op jit(solution)/shard_map/ppermute | solution.py:230
  31.1 0.1 collective-permute-start.10
  31.2 4.5 %collective-permute-start.7 = (bf16[192,384]{1,0:T(8,128)(2,1)S(1)}, bf16[192,384]{1,0:T(8,128)(2,1)S(1)}, u32[]{:S(2)}, u32[]{:S(2)}) collective-permute-start(bf16[192,384]{1,0:T(8,128)(2,1)S(1)} %attend_last.1), channel_id=1, source_target_pairs={{3,0},{10,1},{5,2},{12,3},{7,4},{14,5},{9,6},{0,7},{11,8},{2,9},{1... | collective-permute-start | bytes 442376 | tf_op jit(solution)/shard_map/ppermute | solution.py:216
  35.7 0.0 collective-permute-start.6
  35.7 0.4 collective-permute-start.5
  36.1 6.7 %collective-permute-done.7.refs_3_ = bf16[192,384]{1,0:T(8,128)(2,1)S(1)} collective-permute-done((bf16[192,384]{1,0:T(8,128)(2,1)S(1)}, bf16[192,384]{1,0:T(8,128)(2,1)S(1)}, u32[]{:S(2)}, u32[]{:S(2)}) %collective-permute-start.7) | collective-permute-done | bytes 147488 | tf_op jit(solution)/shard_map/ppermute | solution.py:216
  42.8 1.9 %collective-permute-start.4 = (bf16[192,384]{1,0:T(8,128)(2,1)S(1)}, bf16[192,384]{1,0:T(8,128)(2,1)S(1)}, u32[]{:S(2)}, u32[]{:S(2)}) collective-permute-start(bf16[192,384]{1,0:T(8,128)(2,1)S(1)} %attend_last.1), channel_id=1, source_target_pairs={{0,0},{9,1},{6,2},{15,3},{4,4},{13,5},{10,6},{3,7},{8,8},{1,9},{14... | collective-permute-start | bytes 442376 | tf_op jit(solution)/shard_map/ppermute | solution.py:216
  44.7 0.0 collective-permute-done.6.refs_2_
  44.7 1.1 %collective-permute-done.5.refs_1_ = bf16[192,384]{1,0:T(8,128)(2,1)S(1)} collective-permute-done((bf16[192,384]{1,0:T(8,128)(2,1)S(1)}, bf16[192,384]{1,0:T(8,128)(2,1)S(1)}, u32[]{:S(2)}, u32[]{:S(2)}) %collective-permute-start.5) | collective-permute-done | bytes 147488 | tf_op jit(solution)/shard_map/ppermute | solution.py:216
  45.8 5.3 %collective-permute-done.4.refs_0_ = bf16[192,384]{1,0:T(8,128)(2,1)S(1)} collective-permute-done((bf16[192,384]{1,0:T(8,128)(2,1)S(1)}, bf16[192,384]{1,0:T(8,128)(2,1)S(1)}, u32[]{:S(2)}, u32[]{:S(2)}) %collective-permute-start.4) | collective-permute-done | bytes 147488 | tf_op jit(solution)/shard_map/ppermute | solution.py:216
  51.1 0.0 collective-permute-done.9.refs_5_
  51.1 0.0 collective-permute-done.10.refs_7_
  51.1 2.2 %project.1 = bf16[192,1280]{1,0:T(8,128)(2,1)S(1)} custom-call(bf16[192,384]{1,0:T(8,128)(2,1)S(1)} %collective-permute-done.4.refs_0_, bf16[192,384]{1,0:T(8,128)(2,1)S(1)} %collective-permute-done.5.refs_1_, bf16[192,384]{1,0:T(8,128)(2,1)S(1)} %collective-permute-done.6.refs_2_, bf16[192,384]{1,0:T(8,128)(2,1)S(1)} %collective-permute-done.7.refs_3_, ...), custom_call_target="tpu_custom_call" | custom-call | flops 754974720 | bytes 3932160 | tf_op jit(solution)/shard_map/project/pallas_call | solution.py:120
  53.3 1.9 %collective-permute-start.11 = (bf16[192,1280]{1,0:T(8,128)(2,1)S(1)}, bf16[192,1280]{1,0:T(8,128)(2,1)S(1)}, u32[]{:S(2)}, u32[]{:S(2)}) collective-permute-start(bf16[192,1280]{1,0:T(8,128)(2,1)S(1)} %project.1), channel_id=1, source_target_pairs={{0,0},{1,8},{2,4},{3,12},{4,5},{5,13},{6,9},{7,1},{8,10},{9,2},{10... | collective-permute-start | bytes 1474568 | tf_op jit(solution)/shard_map/ppermute | solution.py:237
  55.2 13.8 %collective-permute-done.11 = bf16[192,1280]{1,0:T(8,128)(2,1)S(1)} collective-permute-done((bf16[192,1280]{1,0:T(8,128)(2,1)S(1)}, bf16[192,1280]{1,0:T(8,128)(2,1)S(1)}, u32[]{:S(2)}, u32[]{:S(2)}) %collective-permute-start.11) | collective-permute-done | bytes 491552 | tf_op jit(solution)/shard_map/ppermute | solution.py:237
  69.1 0.0 copy-done.5
  69.1 1.0 %convert_multiply_fusion = f32[192,1280]{1,0:T(8,128)} fusion(bf16[192,1280]{1,0:T(8,128)(2,1)S(1)} %collective-permute-done.11, f32[1280]{0:T(1024)S(1)} %copy-done.5), kind=kLoop, calls=%fused_computation | loop fusion | flops 491520 | bytes 1479680 | tf_op jit(solution)/shard_map/mul | solution.py:250
  (1 shorter events, 0.0 us)
Async XLA Ops:
  0.0 3.0 %copy-start.4 = (bf16[192,384]{1,0:T(8,128)(2,1)S(1)}, bf16[192,384]{1,0:T(8,128)(2,1)}, u32[]{:S(2)}) copy-start(bf16[192,384]{1,0:T(8,128)(2,1)} %param.11) | copy-start | bytes 442372
  0.0 27.5 %collective-permute-start.8 = (bf16[384,1280]{1,0:T(8,128)(2,1)}, bf16[384,1280]{1,0:T(8,128)(2,1)S(1)}, u32[]{:S(2)}, u32[]{:S(2)}) collective-permute-start(bf16[384,1280]{1,0:T(8,128)(2,1)} %refs_4_), channel_id=1, source_target_pairs={{0,2},{1,3},{2,0},{3,1},{4,6},{5,7},{6,4},{7,5},{8,10},{9,11},{10,... | collective-permute-start | bytes 2949128 | tf_op jit(solution)/shard_map/ppermute | solution.py:198
  2.0 17.7 %copy-start.3 = (bf16[192,384]{1,0:T(8,128)(2,1)S(1)}, bf16[192,384]{1,0:T(8,128)(2,1)}, u32[]{:S(2)}) copy-start(bf16[192,384]{1,0:T(8,128)(2,1)} %value_ref.1) | copy-start | bytes 442372
  3.0 16.7 %copy-start.1 = (bf16[192,384]{1,0:T(8,128)(2,1)S(1)}, bf16[192,384]{1,0:T(8,128)(2,1)}, u32[]{:S(2)}) copy-start(bf16[192,384]{1,0:T(8,128)(2,1)} %q_ref.3) | copy-start | bytes 442372
  3.0 16.7 %copy-start.2 = (bf16[192,384]{1,0:T(8,128)(2,1)S(1)}, bf16[192,384]{1,0:T(8,128)(2,1)}, u32[]{:S(2)}) copy-start(bf16[192,384]{1,0:T(8,128)(2,1)} %key_ref.1) | copy-start | bytes 442372
  3.1 15.2 %collective-permute-start = (bf16[192,768]{1,0:T(8,128)(2,1)S(1)}, bf16[192,768]{1,0:T(8,128)(2,1)S(1)}, u32[]{:S(2)}, u32[]{:S(2)}) collective-permute-start(bf16[192,768]{1,0:T(8,128)(2,1)S(1)} %constant_dynamic-update-slice_fusion), channel_id=1, source_target_pairs={{0,8},{4,12},{8,0},{12,4},{1,9},{5,13},{9,1},{13,5},{2,10},{6,14},... | collective-permute-start | bytes 884744 | tf_op jit(solution)/shard_map/ppermute | solution.py:145
  5.4 14.3 %collective-permute-start.2 = (bf16[192,768]{1,0:T(8,128)(2,1)S(1)}, bf16[192,768]{1,0:T(8,128)(2,1)S(1)}, u32[]{:S(2)}, u32[]{:S(2)}) collective-permute-start(bf16[192,768]{1,0:T(8,128)(2,1)S(1)} %constant_dynamic-update-slice_fusion), channel_id=1, source_target_pairs={{4,0},{8,4},{12,8},{5,1},{9,5},{13,9},{6,2},{10,6},{14,10},{7,3},{... | collective-permute-start | bytes 884744 | tf_op jit(solution)/shard_map/ppermute | solution.py:156
  6.7 13.0 %collective-permute-start.1 = (bf16[192,768]{1,0:T(8,128)(2,1)S(1)}, bf16[192,768]{1,0:T(8,128)(2,1)S(1)}, u32[]{:S(2)}, u32[]{:S(2)}) collective-permute-start(bf16[192,768]{1,0:T(8,128)(2,1)S(1)} %constant_dynamic-update-slice_fusion), channel_id=1, source_target_pairs={{0,4},{4,8},{8,12},{1,5},{5,9},{9,13},{2,6},{6,10},{10,14},{3,7},{... | collective-permute-start | bytes 884744 | tf_op jit(solution)/shard_map/ppermute | solution.py:155
  18.3 7.8 %collective-permute-start.3 = (bf16[192,768]{1,0:T(8,128)(2,1)S(1)}, bf16[192,768]{1,0:T(8,128)(2,1)S(1)}, u32[]{:S(2)}, u32[]{:S(2)}) collective-permute-start(bf16[192,768]{1,0:T(8,128)(2,1)S(1)} %collective-permute-done.refs_0_), channel_id=1, source_target_pairs={{8,12},{4,0},{9,13},{5,1},{10,14},{6,2},{11,15},{7,3},{24,28},{20,... | collective-permute-start | bytes 884744 | tf_op jit(solution)/shard_map/ppermute | solution.py:162
  21.7 5.8 %copy-start = (bf16[384,1280]{1,0:T(8,128)(2,1)S(1)}, bf16[384,1280]{1,0:T(8,128)(2,1)}, u32[]{:S(2)}) copy-start(bf16[384,1280]{1,0:T(8,128)(2,1)} %refs_4_) | copy-start | bytes 2949124
  27.5 41.5 %copy-start.5 = (f32[1280]{0:T(1024)S(1)}, f32[1280]{0:T(1024)}, u32[]{:S(2)}) copy-start(f32[1280]{0:T(1024)} %param.13) | copy-start | bytes 15364
  27.5 23.6 %collective-permute-start.9 = (bf16[384,1280]{1,0:T(8,128)(2,1)S(1)}, bf16[384,1280]{1,0:T(8,128)(2,1)S(1)}, u32[]{:S(2)}, u32[]{:S(2)}) collective-permute-start(bf16[384,1280]{1,0:T(8,128)(2,1)S(1)} %copy-done), channel_id=1, source_target_pairs={{0,1},{1,0},{2,3},{3,2},{4,5},{5,4},{6,7},{7,6},{8,9},{9,8},{10,11... | collective-permute-start | bytes 2949128 | tf_op jit(solution)/shard_map/ppermute | solution.py:230
  31.1 20.1 %collective-permute-start.10 = (bf16[384,1280]{1,0:T(8,128)(2,1)S(1)}, bf16[384,1280]{1,0:T(8,128)(2,1)S(1)}, u32[]{:S(2)}, u32[]{:S(2)}) collective-permute-start(bf16[384,1280]{1,0:T(8,128)(2,1)S(1)} %collective-permute-done.8.refs_6_), channel_id=1, source_target_pairs={{0,1},{1,0},{2,3},{3,2},{4,5},{5,4},{6,7},{7,6},{8,9},{9,8},{10,11... | collective-permute-start | bytes 2949128 | tf_op jit(solution)/shard_map/ppermute | solution.py:230
  31.2 11.6 %collective-permute-start.7 = (bf16[192,384]{1,0:T(8,128)(2,1)S(1)}, bf16[192,384]{1,0:T(8,128)(2,1)S(1)}, u32[]{:S(2)}, u32[]{:S(2)}) collective-permute-start(bf16[192,384]{1,0:T(8,128)(2,1)S(1)} %attend_last.1), channel_id=1, source_target_pairs={{3,0},{10,1},{5,2},{12,3},{7,4},{14,5},{9,6},{0,7},{11,8},{2,9},{1... | collective-permute-start | bytes 442376 | tf_op jit(solution)/shard_map/ppermute | solution.py:216
  35.7 9.0 %collective-permute-start.6 = (bf16[192,384]{1,0:T(8,128)(2,1)S(1)}, bf16[192,384]{1,0:T(8,128)(2,1)S(1)}, u32[]{:S(2)}, u32[]{:S(2)}) collective-permute-start(bf16[192,384]{1,0:T(8,128)(2,1)S(1)} %attend_last.1), channel_id=1, source_target_pairs={{2,0},{11,1},{4,2},{13,3},{6,4},{15,5},{8,6},{1,7},{10,8},{3,9},{1... | collective-permute-start | bytes 442376 | tf_op jit(solution)/shard_map/ppermute | solution.py:216
  35.7 10.1 %collective-permute-start.5 = (bf16[192,384]{1,0:T(8,128)(2,1)S(1)}, bf16[192,384]{1,0:T(8,128)(2,1)S(1)}, u32[]{:S(2)}, u32[]{:S(2)}) collective-permute-start(bf16[192,384]{1,0:T(8,128)(2,1)S(1)} %attend_last.1), channel_id=1, source_target_pairs={{1,0},{8,1},{7,2},{14,3},{5,4},{12,5},{11,6},{2,7},{9,8},{0,9},{15... | collective-permute-start | bytes 442376 | tf_op jit(solution)/shard_map/ppermute | solution.py:216
  42.8 8.4 %collective-permute-start.4 = (bf16[192,384]{1,0:T(8,128)(2,1)S(1)}, bf16[192,384]{1,0:T(8,128)(2,1)S(1)}, u32[]{:S(2)}, u32[]{:S(2)}) collective-permute-start(bf16[192,384]{1,0:T(8,128)(2,1)S(1)} %attend_last.1), channel_id=1, source_target_pairs={{0,0},{9,1},{6,2},{15,3},{4,4},{13,5},{10,6},{3,7},{8,8},{1,9},{14... | collective-permute-start | bytes 442376 | tf_op jit(solution)/shard_map/ppermute | solution.py:216
  53.3 15.7 %collective-permute-start.11 = (bf16[192,1280]{1,0:T(8,128)(2,1)S(1)}, bf16[192,1280]{1,0:T(8,128)(2,1)S(1)}, u32[]{:S(2)}, u32[]{:S(2)}) collective-permute-start(bf16[192,1280]{1,0:T(8,128)(2,1)S(1)} %project.1), channel_id=1, source_target_pairs={{0,0},{1,8},{2,4},{3,12},{4,5},{5,13},{6,9},{7,1},{8,10},{9,2},{10... | collective-permute-start | bytes 1474568 | tf_op jit(solution)/shard_map/ppermute | solution.py:237
